TPU v7x, 128 devices: a whole 4x4x4 slice. The times are simulated.
128 devices in a mesh: net: 8 (over x, core), rep: 16 (over y, z).
Axes of the slice: x: 4, y: 4, z: 4, core: 2. Of those that a mesh axis runs over, the one named last changes fastest.
Arguments:
- latent: bfloat16 [64, 64, 256], P('net', 'rep'), may hold values from -7.2 to 7.2
- hint: bfloat16 [64, 64, 64, 192], P('net', 'rep'), may hold values from -6 to 6
- cond_ids: int32 [64, 1], P('net'), may hold values from 0 to 7; in each aligned block of 8 rows (0 to 7, 8 to 15, ...) at most 2 rows name the same one
- valid: int32 [64], P('net'), may hold values 0 or 1
- cond_scale: float32 [64], P('net'), may hold values from 0.5 to 1.5
- ctl_in: bfloat16 [8, 3, 3, 4, 320], P('net'), may hold values from -1 to 1
- ctl_hint: bfloat16 [8, 192, 320], P('net'), may hold values from -0.4375 to 0.4375
- ctl_zero0: bfloat16 [8, 320, 320], P('net'), may hold values from -0.3125 to 0.3125
- ctl_gain: bfloat16 [8, 320], P('net'), may hold values from 0.099609375 to 1.8984375
- ctl_conv: bfloat16 [8, 3, 3, 320, 320], P('net'), may hold values from -0.109375 to 0.109375
- ctl_zero1: bfloat16 [8, 320, 320], P('net'), may hold values from -0.3125 to 0.3125
- unet_in: bfloat16 [3, 3, 4, 320], replicated, may hold values from -1 to 1
- unet_gain: bfloat16 [320], replicated, may hold values from 0.099609375 to 1.8984375
- unet_conv: bfloat16 [3, 3, 320, 320], replicated, may hold values from -0.109375 to 0.109375
Outputs:
- skip0: bfloat16 [64, 64, 64, 320], P('net', 'rep')
- skip1: bfloat16 [64, 64, 64, 320], P('net', 'rep')
Inputs may be any that keep to these rules, and one draw needn't show every extreme that they name: `cond_ids`: in each aligned block of 8 requests (those of one index of net) no id is named by more than 2 requests.
All inputs are finite; a program needn't handle non-finite values. No bound on the sum of `valid` on one device may be relied on, other than what follows from the above.
Results may differ from a plain program's by a relative error of at most 0.008.
Values may be sent and summed in bfloat16 or wider, within the bound.
A program may use at most 256 MiB of HBM per device.

v0:
```python
import functools

import jax
import jax.numpy as jnp
from jax import lax
from jax.experimental import pallas as pl
from jax.experimental.pallas import tpu as pltpu
from jax.sharding import PartitionSpec as P

MESH = pl.DeviceIdType.MESH
F32, BF16 = jnp.float32, jnp.bfloat16
CH = 320
GROUPS = 32
REQ = 8
EPS = 1e-5
O_M, O_K, O_N, O_Z1, O_Z0, O_ZT, ROWS = 0, 2304, 2880, 3648, 3968, 4288, 4416
CHUNK = 256
E2 = 16 * CHUNK
E2N = ROWS - E2
E2H = E2N // 2
WHR = 256


def gray(v):
    return v + lax.div(v, 2) - 2 * lax.div(v, 3)


def gather_kernel(
    ids, latf, hint, wh, wu, blob, ugain, uconv,
    g, t_out, u_out, h_out, nm_out, nt_out,
    blobv, whs, hintb, latb, lat48, ub, hb, mb, tb, nmb, ntb, ucv, stu, sth,
    s_x, s_yz, s_e, s_wh, s_sib, s_whsib, s_send, s_whsend,
    s_halo, s_hsend, s_st, s_stsend, s_loc, s_out,
):
    net, rep = lax.axis_index("net"), lax.axis_index("rep")
    x, c = lax.div(net, 2), lax.rem(net, 2)
    y, z = lax.div(rep, 4), lax.rem(rep, 4)

    def dev(dx=0, dy=0, dz=0, dc=0):
        return (
            lax.rem(x + dx, 4) * 2 + lax.rem(c + dc, 2),
            lax.rem(y + dy, 4) * 4 + lax.rem(z + dz, 4),
        )

    def rdev(d):
        return (net, lax.rem(rep + d, 16))

    def colour(q, dy=0, dz=0):
        yy, zz = lax.rem(y + dy, 4), lax.rem(z + dz, 4)
        a, b = (yy, zz) if q == 0 else (zz, yy)
        ga, odd = gray(a), lax.rem(b, 2)
        return ga + odd * (3 - 2 * ga)

    def net_of(dx):
        return lax.rem(x + dx, 4) * 2 + c

    loads = [
        pltpu.make_async_copy(blob, blobv, s_loc.at[0]),
        pltpu.make_async_copy(hint, hintb.at[:, pl.ds(1, 4)], s_loc.at[1]),
        pltpu.make_async_copy(uconv, ucv, s_loc.at[2]),
    ]
    for cp in loads:
        cp.start()

    barrier = pltpu.get_barrier_semaphore()
    partners = [
        dev(dx=1), dev(dx=3), dev(dc=1), dev(dy=1), dev(dy=3), dev(dy=2),
        dev(dz=1), dev(dz=3), dev(dz=2), rdev(1), rdev(15),
    ]
    for p in partners:
        pl.semaphore_signal(barrier, inc=1, device_id=p, device_id_type=MESH)
    pl.semaphore_wait(barrier, len(partners))

    def send(src, dst, sem, where, ssem):
        pltpu.make_async_remote_copy(
            src_ref=src, dst_ref=dst, send_sem=ssem, recv_sem=sem,
            device_id=where, device_id_type=MESH,
        ).start()

    def arrived(ref, sem):
        pltpu.make_async_copy(ref, ref, sem).wait()

    EV = {}
    for q in range(2):
        for h in range(2):
            EV["L", q, h] = (3, q, h, q * 2 + h)
            EV["R", q, h] = (1, q, h, 4 + q * 2 + h)
        EV["LL", q] = (2, q, 0, 8 + q)
        EV["RR", q] = (2, q, 1, 10 + q)

    def rows_of(q, h, dy=0, dz=0):
        start = pl.multiple_of((colour(q, dy, dz) * 2 + (q * 8 + h)) * CHUNK, CHUNK)
        return pl.ds(start, CHUNK)

    def own_chunk(q, h):
        r = rows_of(q, h)
        send(blob.at[r], g.at[net, r], s_x.at[EV["L", q, h][3]], dev(dx=1), s_send)
        send(blob.at[r], g.at[net, r], s_x.at[EV["R", q, h][3]], dev(dx=3), s_send)

    def x_relay(key):
        dx, q, h, _ = EV[key]
        ref = g.at[net_of(dx), rows_of(q, h)]
        if key[0] == "L":
            send(ref, ref, s_x.at[EV["LL", q][3]], dev(dx=1), s_send)
        else:
            send(ref, ref, s_x.at[EV["RR", q][3]], dev(dx=3), s_send)

    def to_sib(ref):
        send(ref, ref, s_sib, dev(dc=1), s_send)

    def dirs(q, h):
        main, other = ((0, 1), (2, 3)) if q == 0 else ((2, 3), (0, 1))
        return main + (other[h],)

    STEP = [dict(dy=1), dict(dy=3), dict(dz=1), dict(dz=3)]
    BACK = [dict(dy=3), dict(dy=1), dict(dz=3), dict(dz=1)]

    def x_event(key):
        dx, q, h, sem = EV[key]
        ref = g.at[net_of(dx), rows_of(q, h)]
        arrived(ref, s_x.at[sem])
        for d in dirs(q, h):
            send(ref, ref, s_yz.at[d * 12 + sem], dev(**STEP[d]), s_send)
        to_sib(ref)

    def yz_event(key):
        dx, q, h, sem = EV[key]
        for d in dirs(q, h):
            ref = g.at[net_of(dx), rows_of(q, h, **BACK[d])]
            arrived(ref, s_yz.at[d * 12 + sem])
            to_sib(ref)

    e2r, e2h = pl.ds(E2, E2N), (pl.ds(E2, E2H), pl.ds(E2 + E2H, E2H))

    def own_e2():
        send(blob.at[e2r], g.at[net, e2r], s_e.at[0], dev(dx=1), s_send)
        send(blob.at[e2r], g.at[net, e2r], s_e.at[1], dev(dx=3), s_send)

    def e2_event():
        for i, dx, to in ((0, 3, 1), (1, 1, 3)):
            ref = g.at[net_of(dx), e2r]
            arrived(ref, s_e.at[i])
            half = g.at[net_of(dx), e2h[i]]
            send(half, half, s_e.at[2 + i], dev(dx=to), s_send)
            to_sib(ref)

    def e2_far():
        for i in range(2):
            ref = g.at[net_of(2), e2h[i]]
            arrived(ref, s_e.at[2 + i])
            to_sib(ref)

    whh = (pl.ds(0, WHR // 2), pl.ds(WHR // 2, WHR // 2))

    def wh_sib(ref):
        send(ref, ref, s_whsib, dev(dc=1), s_whsend)

    def wh_event():
        for i, dx, to in ((0, 3, 1), (1, 1, 3)):
            ref = whs.at[net_of(dx)]
            arrived(ref, s_wh.at[i])
            half = whs.at[net_of(dx), whh[i]]
            send(half, half, s_wh.at[2 + i], dev(dx=to), s_whsend)
            wh_sib(ref)

    def wh_far():
        for i in range(2):
            ref = whs.at[net_of(2), whh[i]]
            arrived(ref, s_wh.at[2 + i])
            wh_sib(ref)
        arrived(whs.at[pl.ds(0, 4)], s_whsib)

    halos = [
        (latf, latb.at[0], rdev(1)), (latf, latb.at[1], rdev(15)),
        (hint.at[:, 3], hintb.at[:, 0], rdev(1)), (hint.at[:, 0], hintb.at[:, 5], rdev(15)),
    ]
    for i, (src, dst, to) in enumerate(halos[:2]):
        send(src, dst, s_halo.at[i], to, s_hsend.at[i])
    own_chunk(0, 0)
    own_chunk(1, 0)
    send(wh, whs.at[net], s_wh.at[0], dev(dx=1), s_whsend)
    send(wh, whs.at[net], s_wh.at[1], dev(dx=3), s_whsend)
    send(wh, whs.at[net], s_whsib, dev(dc=1), s_whsend)
    send(blob, g.at[net], s_sib, dev(dc=1), s_send)
    for i, (src, dst, to) in enumerate(halos):
        if i >= 2:
            send(src, dst, s_halo.at[i], to, s_hsend.at[i])
    own_wh = pltpu.make_async_copy(wh, whs.at[net], s_loc.at[3])
    own_wh.start()
    loads[0].wait()
    own_blob = pltpu.make_async_copy(blobv, g.at[net], s_loc.at[4])
    own_blob.start()

    for i in range(2):
        arrived(latb.at[i], s_halo.at[i])
    li = lax.broadcasted_iota(jnp.int32, (256, 256), 0)
    lj = lax.broadcasted_iota(jnp.int32, (256, 256), 1)
    perm = (lj == (252 - (li - lax.rem(li, 4)) + lax.rem(li, 4))).astype(BF16)
    above = jnp.where(rep > 0, latb[0, 16:32, :], 0.0)
    below = jnp.where(rep < 15, latb[1, 0:16, :], 0.0)
    latall = jnp.concatenate([above, latf[...], below], axis=0).astype(BF16)
    latb[2, :, :] = jnp.dot(latall, perm, preferred_element_type=F32)[0:32]
    latb[3, :, :] = jnp.dot(latall, perm, preferred_element_type=F32)[32:64]

    xs = lax.broadcasted_iota(jnp.int32, (64, 128), 0)
    ls = lax.broadcasted_iota(jnp.int32, (64, 128), 1)
    keep = (ls < 12) & ~((ls < 4) & (xs == 63)) & ~((ls >= 8) & (xs == 0))

    def lat_step(b, _):
        rolled = []
        for r in range(8):
            row = latb[2 + r // 4, pl.ds((r % 4) * 8 + b, 1), :]
            skew = pltpu.roll(jnp.broadcast_to(row, (8, 256)), 0, 1, stride=4, stride_axis=0)
            full = [pltpu.roll(skew, 8 + 32 * k, 1)[:, :128] for k in range(8)]
            rolled.append(jnp.where(keep, jnp.concatenate(full, axis=0), 0.0))
        for r in range(6):
            v = rolled[r] + pltpu.roll(rolled[r + 1], 16, 1) + pltpu.roll(rolled[r + 2], 32, 1)
            lat48[b, pl.ds(r * 64, 64), :] = v.astype(BF16)
        return 0

    lax.fori_loop(0, REQ, lat_step, 0)

    def sums(st, b, v):
        f = v[64:320].astype(F32)
        st[pl.ds(b, 1), :] = jnp.sum(f, axis=0, keepdims=True)
        st[pl.ds(8 + b, 1), :] = jnp.sum(f * f, axis=0, keepdims=True)

    def u_step(b, _):
        v = jnp.dot(lat48[b, :, 0:48], wu[...], preferred_element_type=F32).astype(BF16)
        ub[b] = v
        sums(stu.at[0], b, v)
        pltpu.make_async_copy(ub.at[b, pl.ds(64, 256)], u_out.at[b], s_out.at[0, b]).start()
        return 0

    lax.fori_loop(0, REQ, u_step, 0)

    x_event(("L", 0, 0))
    x_event(("R", 0, 0))
    own_chunk(0, 1)

    def stats_send(st, base, k, axis):
        for j in range(1, 4):
            send(st.at[k], st.at[k + j], s_st.at[base + k + j], dev(**{axis: j}), s_stsend.at[base + k + j])

    def stats_sum(st, base, k):
        total = st[k]
        for j in range(1, 4):
            arrived(st.at[k + j], s_st.at[base + k + j])
            total = total + st[k + j]
        return total

    stats_send(stu, 0, 0, "dz")
    x_event(("L", 1, 0))
    x_event(("R", 1, 0))
    own_chunk(1, 1)
    stu[4] = stats_sum(stu, 0, 0)
    yz_event(("L", 0, 0))
    yz_event(("R", 0, 0))
    stats_send(stu, 0, 4, "dy")
    wh_event()
    x_relay(("L", 0, 0))
    x_relay(("L", 1, 0))

    gi = lax.broadcasted_iota(jnp.int32, (CH, CH), 0)
    gj = lax.broadcasted_iota(jnp.int32, (CH, CH), 1)
    gsz = CH // GROUPS
    same = (lax.div(gi, gsz) == lax.div(gj, gsz)).astype(F32)

    def stats_final(st, base):
        total = stats_sum(st, base, 4)
        per = jnp.dot(total, same, preferred_element_type=F32, precision=lax.Precision.HIGHEST)
        per = per * (1.0 / (64 * 64 * gsz))
        m, q = per[0:8], per[8:16]
        st[8, 0:8, :] = m
        st[8, 8:16, :] = lax.rsqrt(q - m * m + EPS)

    pos = lax.broadcasted_iota(jnp.int32, (384, CH), 0)
    col = lax.rem(pos, 64)
    inside = ((pos >= 64) | (rep > 0)) & ((pos < 320) | (rep < 15))

    def normed(v, st, b, gain):
        m = st[8, pl.ds(b, 1), :]
        s = st[8, pl.ds(8 + b, 1), :] * gain
        n = (v.astype(F32) - m) * s
        n = n / (1.0 + jnp.exp(-n))
        n = jnp.where(inside, n, 0.0)
        left = jnp.where(col == 0, 0.0, pltpu.roll(n, 1, 0))
        right = jnp.where(col == 63, 0.0, pltpu.roll(n, 383, 0))
        return left, n, right

    x_event(("L", 0, 1))
    x_event(("R", 0, 1))
    x_relay(("R", 0, 1))
    stats_final(stu, 0)

    def m_step(b, _):
        for i, v in enumerate(normed(ub[b], stu, b, ugain[...].astype(F32))):
            mb[b, i] = v.astype(BF16)
        return 0

    lax.fori_loop(0, REQ, m_step, 0)

    loads[2].wait()

    def conv_step(b):
        acc = ub[b, 64:320, :].astype(F32)
        for i in range(3):
            for j in range(3):
                acc = acc + jnp.dot(
                    mb[b, j, pl.ds(i * 64, 256), :], ucv[i, j], preferred_element_type=F32
                )
        tb[b] = acc
        pltpu.make_async_copy(tb.at[b], t_out.at[b], s_out.at[2, b]).start()

    after = {
        0: [lambda: yz_event(("L", 1, 0)), lambda: yz_event(("R", 1, 0))],
        1: [lambda: x_event(("L", 1, 1)), lambda: x_event(("R", 1, 1)), lambda: x_relay(("R", 1, 1)), own_e2],
        3: [lambda: yz_event(("L", 0, 1)), lambda: yz_event(("R", 0, 1))],
        5: [wh_far],
    }

    def loop_a(b, _):
        conv_step(b)
        for k, todo in after.items():
            @pl.when(b == k)
            def _():
                for f in todo:
                    f()
        return 0

    lax.fori_loop(0, REQ, loop_a, 0)

    loads[1].wait()
    own_wh.wait()
    for i in range(2, 4):
        arrived(hintb.at[:, 0], s_halo.at[i])

    def h_step(b, _):
        n = ids[b, 0]
        w = whs[n]
        v = jnp.dot(hintb[b].reshape(384, 192), w[0:192], preferred_element_type=F32)
        v = v + jnp.dot(lat48[b, :, 0:48], w[192:240], preferred_element_type=F32)
        v = v.astype(BF16)
        hb[b] = v
        sums(sth.at[0], b, v)
        pltpu.make_async_copy(hb.at[b, pl.ds(64, 256)], h_out.at[b], s_out.at[1, b]).start()
        return 0

    lax.fori_loop(0, REQ, h_step, 0)

    x_event(("LL", 0))
    x_event(("RR", 0))
    stats_send(sth, 8, 0, "dz")
    yz_event(("L", 1, 1))
    yz_event(("R", 1, 1))
    sth[4] = stats_sum(sth, 8, 0)
    x_event(("LL", 1))
    x_event(("RR", 1))
    stats_send(sth, 8, 4, "dy")
    e2_event()
    stats_final(sth, 8)

    def n_step(b, _):
        n = ids[b, 0]
        gain = whs[n, 240:256, :][0:1].astype(F32)
        parts = [v.astype(BF16) for v in normed(hb[b], sth, b, gain)]
        for i, v in enumerate(parts):
            nmb[b, i] = v[:, 0:256]
        ntb[b] = jnp.concatenate([v[:, 256:320] for v in parts], axis=1)
        pltpu.make_async_copy(nmb.at[b], nm_out.at[b], s_out.at[3, b]).start()
        pltpu.make_async_copy(ntb.at[b], nt_out.at[b], s_out.at[4, b]).start()
        @pl.when(b == 3)
        def _():
            yz_event(("LL", 0))
            yz_event(("RR", 0))
            e2_far()
        return 0

    lax.fori_loop(0, REQ, n_step, 0)
    yz_event(("LL", 1))
    yz_event(("RR", 1))

    arrived(g.at[pl.ds(0, 4)], s_sib)
    arrived(g.at[pl.ds(0, 7)], s_send)
    arrived(whs.at[pl.ds(0, 7)], s_whsend)
    own_blob.wait()
    for i in range(4):
        src = halos[i][0]
        pltpu.make_async_copy(src, src, s_hsend.at[i]).wait()
    for base, st in ((0, stu), (8, sth)):
        for k in (0, 4):
            for j in range(1, 4):
                arrived(st.at[k], s_stsend.at[base + k + j])

    def out_step(b, _):
        outs = (
            (ub.at[b, pl.ds(64, 256)], u_out), (hb.at[b, pl.ds(64, 256)], h_out),
            (tb.at[b], t_out), (nmb.at[b], nm_out), (ntb.at[b], nt_out),
        )
        for i, (src, dst) in enumerate(outs):
            pltpu.make_async_copy(src, dst.at[b], s_out.at[i, b]).wait()
        return 0

    lax.fori_loop(0, REQ, out_step, 0)


def gather_call(ids, latf, hint, wh, wu, blob, ugain, uconv):
    hbm = pl.BlockSpec(memory_space=pl.ANY)
    vm = pl.BlockSpec(memory_space=pltpu.VMEM)
    sm = pl.BlockSpec(memory_space=pltpu.SMEM)
    dma = pltpu.SemaphoreType.DMA
    return pl.pallas_call(
        gather_kernel,
        out_shape=(
            jax.ShapeDtypeStruct((8, ROWS, 256), BF16),
            jax.ShapeDtypeStruct((REQ, 256, CH), F32),
            jax.ShapeDtypeStruct((REQ, 256, CH), BF16),
            jax.ShapeDtypeStruct((REQ, 256, CH), BF16),
            jax.ShapeDtypeStruct((REQ, 3, 384, 256), BF16),
            jax.ShapeDtypeStruct((REQ, 384, 192), BF16),
        ),
        in_specs=[sm, vm, hbm, vm, vm, hbm, vm, hbm],
        out_specs=(hbm,) * 6,
        scratch_shapes=[
            pltpu.VMEM((ROWS, 256), BF16),
            pltpu.VMEM((8, WHR, CH), BF16),
            pltpu.VMEM((REQ, 6, 64, 192), BF16),
            pltpu.VMEM((4, 32, 256), F32),
            pltpu.VMEM((REQ, 384, 128), BF16),
            pltpu.VMEM((REQ, 384, CH), BF16),
            pltpu.VMEM((REQ, 384, CH), BF16),
            pltpu.VMEM((REQ, 3, 384, CH), BF16),
            pltpu.VMEM((REQ, 256, CH), F32),
            pltpu.VMEM((REQ, 3, 384, 256), BF16),
            pltpu.VMEM((REQ, 384, 192), BF16),
            pltpu.VMEM((3, 3, CH, CH), BF16),
            pltpu.VMEM((9, 16, CH), F32),
            pltpu.VMEM((9, 16, CH), F32),
            dma((12,)), dma((48,)), dma((4,)), dma((4,)), dma, dma, dma, dma,
            dma((4,)), dma((4,)), dma((16,)), dma((16,)), dma((5,)), dma((5, REQ)),
        ],
        compiler_params=pltpu.CompilerParams(
            collective_id=0, has_side_effects=True, vmem_limit_bytes=60 << 20
        ),
        name="gather",
    )(ids, latf, hint, wh, wu, blob, ugain, uconv)


def control_kernel(ids, scale, valid, wb, nm, nt, hb, ub, tb, o0, o1):
    b = pl.program_id(0)
    w = scale[b] * valid[b].astype(F32)

    def dot(a, k):
        return jnp.dot(a, k, preferred_element_type=F32)

    def proj(h, zm, lane, ktail):
        ha, hc, ht = h[:, 0:128], h[:, 128:256], h[:, 256:320]
        main = dot(h[:, 0:256], wb[0, zm : zm + 256, :]) + dot(ht, wb[0, zm + 256 : zm + 320, :])
        zt = wb[0, O_ZT : O_ZT + 128, :]
        tail = dot(ha, zt[:, lane : lane + 64]) + dot(hc, zt[:, 128 + lane : 192 + lane]) + dot(ht, ktail)
        return jnp.concatenate([main, tail], axis=1).astype(BF16).astype(F32)

    h0 = hb[0]
    r0 = proj(h0, O_Z0, 0, wb[0, O_N + 192 : O_N + 256, 192:256])
    o0[0] = (ub[0].astype(F32) + w * r0).astype(BF16).reshape(4, 64, CH)

    main = jnp.zeros((256, 256), F32)
    side = jnp.zeros((256, 192), F32)
    tail = jnp.zeros((256, 64), F32)
    for i in range(3):
        rows = slice(i * 64, i * 64 + 256)
        for j in range(3):
            k = O_M + (i * 3 + j) * 256
            main = main + dot(nm[0, j, rows, :], wb[0, k : k + 256, :])
        k, n = O_K + i * 192, O_N + i * 256
        main = main + dot(nt[0, rows, :], wb[0, k : k + 192, :])
        side = side + dot(nm[0, 1, rows, :], wb[0, n : n + 256, 0:192])
        tail = tail + dot(nt[0, rows, :], wb[0, n : n + 192, 192:256])
    col = lax.rem(lax.broadcasted_iota(jnp.int32, (256, 64), 0), 64)
    left = jnp.where(col == 0, 0.0, pltpu.roll(side[:, 0:64], 1, 0))
    right = jnp.where(col == 63, 0.0, pltpu.roll(side[:, 128:192], 255, 0))
    tail = tail + left + side[:, 64:128] + right
    h1 = (h0.astype(F32) + jnp.concatenate([main, tail], axis=1)).astype(BF16)
    r1 = proj(h1, O_Z1, 64, wb[0, O_N + 448 : O_N + 512, 192:256])
    o1[0] = (tb[0] + w * r1).astype(BF16).reshape(4, 64, CH)


def control_call(ids, scale, valid, g, nm, nt, hb, ub, tb):
    def mine(shape):
        zeros = (0,) * (len(shape) - 1)
        return pl.BlockSpec(shape, lambda b, *_: (b,) + zeros)

    out = jax.ShapeDtypeStruct((REQ, 4, 64, CH), BF16)
    return pl.pallas_call(
        control_kernel,
        out_shape=(out, out),
        grid_spec=pltpu.PrefetchScalarGridSpec(
            num_scalar_prefetch=3,
            grid=(REQ,),
            in_specs=[
                pl.BlockSpec((1, ROWS, 256), lambda b, ids, *_: (ids[b], 0, 0)),
                mine((1, 3, 384, 256)),
                mine((1, 384, 192)),
                mine((1, 256, CH)),
                mine((1, 256, CH)),
                mine((1, 256, CH)),
            ],
            out_specs=[mine((1, 4, 64, CH)), mine((1, 4, 64, CH))],
        ),
        compiler_params=pltpu.CompilerParams(
            dimension_semantics=("arbitrary",), vmem_limit_bytes=60 << 20
        ),
        name="control",
    )(ids, scale, valid, g, nm, nt, hb, ub, tb)


def input_rows(w):
    w = jnp.flip(w, axis=1).reshape(3, 12, CH)
    return jnp.pad(w, ((0, 0), (0, 4), (0, 0))).reshape(48, CH)


def pack(conv, z0, z1):
    m, t = slice(0, 256), slice(256, CH)
    wm = conv[:, :, m, m].reshape(2304, 256)
    wk = conv[:, :, t, m].reshape(576, 256)
    wn = conv[:, :, m, t].transpose(0, 2, 1, 3).reshape(3, 256, 192)
    kt = conv[:, :, t, t].reshape(3, 192, 64)
    zk = jnp.stack([z0[t, t], z1[t, t], jnp.zeros((64, 64), BF16)])
    last = jnp.concatenate([kt, zk], axis=1)
    wn = jnp.concatenate([wn, last], axis=2).reshape(768, 256)
    zt = jnp.concatenate([z0[m, t], z1[m, t]], axis=1).reshape(2, 128, 128)
    zt = jnp.concatenate([zt[0], zt[1]], axis=1)
    return jnp.concatenate([wm, wk, wn, z1[:, m], z0[:, m], zt], axis=0)


def shards(
    latent, hint, cond_ids, valid, cond_scale,
    ctl_in, ctl_hint, ctl_zero0, ctl_gain, ctl_conv, ctl_zero1,
    unet_in, unet_gain, unet_conv,
):
    latf = latent.astype(F32).transpose(1, 0, 2).reshape(32, 256)
    wh = jnp.concatenate(
        [ctl_hint[0], input_rows(ctl_in[0]), ctl_gain, jnp.zeros((15, CH), BF16)], axis=0
    )
    blob = pack(ctl_conv[0], ctl_zero0[0], ctl_zero1[0])
    g, t, u, h, nm, nt = gather_call(
        cond_ids, latf, hint, wh, input_rows(unet_in), blob, unet_gain[None], unet_conv
    )
    return control_call(cond_ids[:, 0], cond_scale, valid, g, nm, nt, h, u, t)


def solution(mesh):
    n, r = "net", "rep"
    return jax.shard_map(
        shards,
        mesh=mesh,
        in_specs=(
            P(n, r, None), P(n, r, None, None), P(n, None), P(n), P(n),
            P(n, None, None, None, None), P(n, None, None), P(n, None, None), P(n, None),
            P(n, None, None, None, None), P(n, None, None), P(), P(), P(),
        ),
        out_specs=(P(n, r, None, None), P(n, r, None, None)),
        check_vma=False,
    )
```

profile of v0, /device:TPU:1, one launch (start us, length us, event | category | flops | bytes accessed | tf_op | source)
XLA Modules:
  0.0 106.3 jit_solution(15552375799108802259)
XLA Ops:
  0.8 1.4 %broadcast_in_dim.7.ugain = bf16[1,320]{1,0:T(2,128)(2,1)} reshape(bf16[320]{0:T(512)(128)(2,1)} %param.26) | data formatting | bytes 1280 | tf_op jit(solution)/shard_map/broadcast_in_dim | solution.py:547
  2.2 1.3 %copy.22.ids = s32[8,1]{1,0:T(8,128)} copy(s32[8,1]{0,1:T(1,128)} %param.16) | data formatting | bytes 64 | tf_op args[2]
  3.5 0.8 rev.7
  4.3 0.8 rev.8
  5.1 0.6 pad.8
  5.7 0.7 convert_bitcast_fusion
  6.5 0.6 copy.26
  7.1 0.7 slice_bitcast_fusion.1
  7.8 0.8 slice.58
  8.7 0.8 slice.59
  9.5 0.1 fusion.2
  9.6 0.9 slice.53
  10.5 0.8 maximum_maximum_fusion.1
  11.4 1.7 %maximum_maximum_fusion.wh = bf16[256,320]{1,0:T(8,128)(2,1)} fusion(bf16[1,320]{1,0:T(2,128)(2,1)} %param.22, bf16[48,320]{1,0:T(8,128)(2,1)S(1)} %bitcast.38, bf16[192,320]{1,0:T(8,128)(2,1)} %bitcast.39, bf16[256]{0:T(256)(128)(2,1)S(1)} %pad.22.clone), kind=kLoop, calls=%fused_computation.2 | loop fusion | flops 655360 | bytes 318592 | tf_op jit(solution)/shard_map/concatenate | solution.py:542
  13.1 1.7 %slice.51 = bf16[3,3,64,256]{3,2,1,0:T(8,128)(2,1)} slice(bf16[3,3,320,320]{3,2,1,0:T(8,128)(2,1)} %bitcast.25), slice={[0:3], [0:3], [256:320], [0:256]} | slice | bytes 589824 | tf_op jit(solution)/shard_map/slice | solution.py:525
  14.8 0.1 slice_bitcast_fusion
  14.9 0.5 copy.23
  15.4 0.4 reshape.52
  16.0 0.7 copy-done.2
  16.8 0.2 maximum_dynamic-update-slice_fusion
  17.1 0.1 fusion.1.blob
  17.2 1.4 %copy-done = bf16[4416,256]{1,0:T(8,128)(2,1)} copy-done((bf16[4416,256]{1,0:T(8,128)(2,1)}, bf16[4416,256]{1,0:T(8,128)(2,1)S(1)}, u32[]{:S(2)}) %copy-start) | copy-done | bytes 2261016
  18.6 71.3 %gather.1 = (bf16[8,4416,256]{2,1,0:T(8,128)(2,1)}, f32[8,256,320]{2,1,0:T(8,128)}, bf16[8,256,320]{2,1,0:T(8,128)(2,1)}, bf16[8,256,320]{2,1,0:T(8,128)(2,1)}, ...) custom-call(s32[8,1]{1,0:T(8,128)} %copy.22.ids, f32[32,256]{1,0:T(8,128)} %bitcast.40, ...), custom_call_target="tpu_custom_call" | custom-call | tf_op jit(solution)/shard_map/gather/pallas_call | solution.py:412
  89.9 16.4 %control.1 = (bf16[8,4,64,320]{3,2,1,0:T(8,128)(2,1)}, bf16[8,4,64,320]{3,2,1,0:T(8,128)(2,1)}) custom-call(s32[8]{0:T(128)} %bitcast.42, f32[8]{0:T(128)} %scale.1, s32[8]{0:T(128)} %valid.1, bf16[8,4416,256]{2,1,0:T(8,128)(2,1)} %get-tuple-element.8.wb, bf16[8,3,384,256]{3,2,1,0:T(8,128)(2,1)} %get-tuple-element.9.nm, ...), custom_call_target="tpu_custom_call" | custom-call | tf_op jit(solution)/shard_map/control/pallas_call | solution.py:494
  (22 shorter events, 0.6 us)
Async XLA Ops:
  0.6 14.1 %copy-start.1 = (bf16[1,3,3,320,320]{4,3,2,1,0:T(8,128)(2,1)S(1)}, bf16[1,3,3,320,320]{4,3,2,1,0:T(8,128)(2,1)}, u32[]{:S(2)}) copy-start(bf16[1,3,3,320,320]{4,3,2,1,0:T(8,128)(2,1)} %param.23) | copy-start | bytes 5529604
  15.8 1.0 copy-start.2
  15.8 1.0 copy-start.3
  15.9 1.1 %copy-start.4 = (bf16[1,320,320]{2,1,0:T(8,128)(2,1)S(1)}, bf16[1,320,320]{2,1,0:T(8,128)(2,1)}, u32[]{:S(2)}) copy-start(bf16[1,320,320]{2,1,0:T(8,128)(2,1)} %param.24) | copy-start | bytes 614404
  15.9 1.2 %copy-start.5 = (bf16[1,320,320]{2,1,0:T(8,128)(2,1)S(1)}, bf16[1,320,320]{2,1,0:T(8,128)(2,1)}, u32[]{:S(2)}) copy-start(bf16[1,320,320]{2,1,0:T(8,128)(2,1)} %param.21) | copy-start | bytes 614404
  17.2 1.4 %copy-start = (bf16[4416,256]{1,0:T(8,128)(2,1)}, bf16[4416,256]{1,0:T(8,128)(2,1)S(1)}, u32[]{:S(2)}) copy-start(bf16[4416,256]{1,0:T(8,128)(2,1)S(1)} %fusion.1.blob) | copy-start | bytes 6782980
where the time goes:
time: 107 us; the launch traced here: 106 us
  Pallas kernels  87.6 us (82%)
  local copies, waits for them, and re-layouts  14.2 us (13%)
  other arithmetic  3.6 us (3%)
    pallas_call x1, Pallas kernels, gather_call(): pl.pallas_call(gather_kernel, out_shape=(jax.ShapeDtypeStruct((8, ROWS, 2...  71.3 us
    pallas_call x1, Pallas kernels, control_call(): pl.pallas_call(control_kernel, out_shape=(out, out), grid_spec=pltpu.Pref...  16.4 us
    unnamed x17, local copies, waits for them, and re-layouts  3.7 us

commit v1 on v0

--- a/solution.py
+++ b/solution.py
@@ -26,9 +26,9 @@
 
 
 def gather_kernel(
-    ids, latf, hint, wh, wu, blob, ugain, uconv,
+    ids, lat, hint, cin, chint, cgain, conv, z0, z1, uin, ugain, uconv,
     g, t_out, u_out, h_out, nm_out, nt_out,
-    blobv, whs, hintb, latb, lat48, ub, hb, mb, tb, nmb, ntb, ucv, stu, sth,
+    blob, whs, cv, z0v, z1v, wu, hintb, latb, lat48, ub, hb, mb, tb, nmb, ntb, ucv, stu, sth,
     s_x, s_yz, s_e, s_wh, s_sib, s_whsib, s_send, s_whsend,
     s_halo, s_hsend, s_st, s_stsend, s_loc, s_out,
 ):
@@ -53,14 +53,6 @@
 
     def net_of(dx):
         return lax.rem(x + dx, 4) * 2 + c
-
-    loads = [
-        pltpu.make_async_copy(blob, blobv, s_loc.at[0]),
-        pltpu.make_async_copy(hint, hintb.at[:, pl.ds(1, 4)], s_loc.at[1]),
-        pltpu.make_async_copy(uconv, ucv, s_loc.at[2]),
-    ]
-    for cp in loads:
-        cp.start()
 
     barrier = pltpu.get_barrier_semaphore()
     partners = [
@@ -69,6 +61,48 @@
     ]
     for p in partners:
         pl.semaphore_signal(barrier, inc=1, device_id=p, device_id_type=MESH)
+
+    loads = [
+        pltpu.make_async_copy(conv.at[0], cv, s_loc.at[0]),
+        pltpu.make_async_copy(z0.at[0], z0v, s_loc.at[1]),
+        pltpu.make_async_copy(z1.at[0], z1v, s_loc.at[2]),
+        pltpu.make_async_copy(chint.at[0], whs.at[net, pl.ds(0, 192)], s_loc.at[3]),
+        pltpu.make_async_copy(hint, hintb.at[:, pl.ds(1, 4)], s_loc.at[4]),
+        pltpu.make_async_copy(uconv, ucv, s_loc.at[5]),
+    ]
+    for cp in loads:
+        cp.start()
+
+    def input_rows(block):
+        parts = [block[i].astype(F32) for i in (2, 1, 0)] + [jnp.zeros((4, CH), F32)]
+        return jnp.concatenate(parts, axis=0).astype(BF16)
+
+    for i in range(3):
+        whs[net, 192 + 16 * i : 208 + 16 * i, :] = input_rows(cin[0, i])
+        wu[16 * i : 16 * i + 16, :] = input_rows(uin[i])
+    whs[net, 240:256, :] = jnp.broadcast_to(cgain[...].astype(F32), (16, CH)).astype(BF16)
+
+    for cp in loads[:3]:
+        cp.wait()
+    for i in range(3):
+        for j in range(3):
+            k = i * 3 + j
+            blob[O_M + k * 256 : O_M + k * 256 + 256, :] = cv[i, j, 0:256, 0:256]
+            blob[O_K + k * 64 : O_K + k * 64 + 64, :] = cv[i, j, 256:CH, 0:256]
+        n = O_N + i * 256
+        if i < 2:
+            zk = (z0v, z1v)[i][256:CH, 256:CH]
+        else:
+            zk = jnp.zeros((64, 64), BF16)
+        kt = jnp.concatenate([cv[i, j, 256:CH, 256:CH] for j in range(3)] + [zk], axis=0)
+        nt = [cv[i, j, 0:256, 256:CH] for j in range(3)]
+        blob[n : n + 256, :] = jnp.concatenate(nt + [kt], axis=1)
+    blob[O_Z1 : O_Z1 + CH, :] = z1v[:, 0:256]
+    blob[O_Z0 : O_Z0 + CH, :] = z0v[:, 0:256]
+    zt = [zv[k : k + 128, 256:CH] for k in (0, 128) for zv in (z0v, z1v)]
+    blob[O_ZT : O_ZT + 128, :] = jnp.concatenate(zt, axis=1)
+    loads[3].wait()
+
     pl.semaphore_wait(barrier, len(partners))
 
     def send(src, dst, sem, where, ssem):
@@ -171,24 +205,22 @@
         arrived(whs.at[pl.ds(0, 4)], s_whsib)
 
     halos = [
-        (latf, latb.at[0], rdev(1)), (latf, latb.at[1], rdev(15)),
+        (lat, latb.at[0], rdev(1)), (lat, latb.at[1], rdev(15)),
         (hint.at[:, 3], hintb.at[:, 0], rdev(1)), (hint.at[:, 0], hintb.at[:, 5], rdev(15)),
     ]
     for i, (src, dst, to) in enumerate(halos[:2]):
         send(src, dst, s_halo.at[i], to, s_hsend.at[i])
     own_chunk(0, 0)
     own_chunk(1, 0)
-    send(wh, whs.at[net], s_wh.at[0], dev(dx=1), s_whsend)
-    send(wh, whs.at[net], s_wh.at[1], dev(dx=3), s_whsend)
-    send(wh, whs.at[net], s_whsib, dev(dc=1), s_whsend)
+    mine = whs.at[net]
+    send(mine, mine, s_wh.at[0], dev(dx=1), s_whsend)
+    send(mine, mine, s_wh.at[1], dev(dx=3), s_whsend)
+    send(mine, mine, s_whsib, dev(dc=1), s_whsend)
     send(blob, g.at[net], s_sib, dev(dc=1), s_send)
     for i, (src, dst, to) in enumerate(halos):
         if i >= 2:
             send(src, dst, s_halo.at[i], to, s_hsend.at[i])
-    own_wh = pltpu.make_async_copy(wh, whs.at[net], s_loc.at[3])
-    own_wh.start()
-    loads[0].wait()
-    own_blob = pltpu.make_async_copy(blobv, g.at[net], s_loc.at[4])
+    own_blob = pltpu.make_async_copy(blob, g.at[net], s_loc.at[6])
     own_blob.start()
 
     for i in range(2):
@@ -196,20 +228,18 @@
     li = lax.broadcasted_iota(jnp.int32, (256, 256), 0)
     lj = lax.broadcasted_iota(jnp.int32, (256, 256), 1)
     perm = (lj == (252 - (li - lax.rem(li, 4)) + lax.rem(li, 4))).astype(BF16)
-    above = jnp.where(rep > 0, latb[0, 16:32, :], 0.0)
-    below = jnp.where(rep < 15, latb[1, 0:16, :], 0.0)
-    latall = jnp.concatenate([above, latf[...], below], axis=0).astype(BF16)
-    latb[2, :, :] = jnp.dot(latall, perm, preferred_element_type=F32)[0:32]
-    latb[3, :, :] = jnp.dot(latall, perm, preferred_element_type=F32)[32:64]
-
     xs = lax.broadcasted_iota(jnp.int32, (64, 128), 0)
     ls = lax.broadcasted_iota(jnp.int32, (64, 128), 1)
     keep = (ls < 12) & ~((ls < 4) & (xs == 63)) & ~((ls >= 8) & (xs == 0))
 
     def lat_step(b, _):
         rolled = []
+        above = jnp.where(rep > 0, latb[0, b].astype(F32)[2:4], 0.0)
+        below = jnp.where(rep < 15, latb[1, b].astype(F32)[0:2], 0.0)
+        rows = jnp.concatenate([above, lat[b].astype(F32), below], axis=0).astype(BF16)
+        rows = jnp.dot(rows, perm, preferred_element_type=F32)
         for r in range(8):
-            row = latb[2 + r // 4, pl.ds((r % 4) * 8 + b, 1), :]
+            row = rows[r : r + 1]
             skew = pltpu.roll(jnp.broadcast_to(row, (8, 256)), 0, 1, stride=4, stride_axis=0)
             full = [pltpu.roll(skew, 8 + 32 * k, 1)[:, :128] for k in range(8)]
             rolled.append(jnp.where(keep, jnp.concatenate(full, axis=0), 0.0))
@@ -234,10 +264,6 @@
 
     lax.fori_loop(0, REQ, u_step, 0)
 
-    x_event(("L", 0, 0))
-    x_event(("R", 0, 0))
-    own_chunk(0, 1)
-
     def stats_send(st, base, k, axis):
         for j in range(1, 4):
             send(st.at[k], st.at[k + j], s_st.at[base + k + j], dev(**{axis: j}), s_stsend.at[base + k + j])
@@ -250,16 +276,14 @@
         return total
 
     stats_send(stu, 0, 0, "dz")
+    x_event(("L", 0, 0))
+    x_event(("R", 0, 0))
+    own_chunk(0, 1)
+    stu[4] = stats_sum(stu, 0, 0)
     x_event(("L", 1, 0))
+    stats_send(stu, 0, 4, "dy")
     x_event(("R", 1, 0))
     own_chunk(1, 1)
-    stu[4] = stats_sum(stu, 0, 0)
-    yz_event(("L", 0, 0))
-    yz_event(("R", 0, 0))
-    stats_send(stu, 0, 4, "dy")
-    wh_event()
-    x_relay(("L", 0, 0))
-    x_relay(("L", 1, 0))
 
     gi = lax.broadcasted_iota(jnp.int32, (CH, CH), 0)
     gj = lax.broadcasted_iota(jnp.int32, (CH, CH), 1)
@@ -288,19 +312,42 @@
         right = jnp.where(col == 63, 0.0, pltpu.roll(n, 383, 0))
         return left, n, right
 
-    x_event(("L", 0, 1))
-    x_event(("R", 0, 1))
-    x_relay(("R", 0, 1))
+    def run(todo):
+        for name, key in todo:
+            if name == "x":
+                x_event(key)
+            elif name == "yz":
+                yz_event(key)
+            elif name == "relay":
+                x_relay(key)
+            else:
+                key()
+
+    def loop(first, last, piece, after):
+        def body(b, _):
+            piece(b)
+            for k, todo in after.items():
+                @pl.when(b == k)
+                def _():
+                    run(todo)
+            return 0
+
+        lax.fori_loop(first, last, body, 0)
+
+    run([("yz", ("L", 0, 0))])
     stats_final(stu, 0)
 
-    def m_step(b, _):
-        for i, v in enumerate(normed(ub[b], stu, b, ugain[...].astype(F32))):
+    def m_step(b):
+        for i, v in enumerate(normed(ub[b], stu, b, ugain[...].astype(F32).reshape(1, CH))):
             mb[b, i] = v.astype(BF16)
-        return 0
-
-    lax.fori_loop(0, REQ, m_step, 0)
-
-    loads[2].wait()
+
+    loop(0, REQ, m_step, {
+        2: [("yz", ("R", 0, 0))],
+        4: [("wh", wh_event), ("relay", ("L", 0, 0)), ("relay", ("L", 1, 0))],
+        7: [("yz", ("L", 1, 0))],
+    })
+
+    loads[5].wait()
 
     def conv_step(b):
         acc = ub[b, 64:320, :].astype(F32)
@@ -312,31 +359,20 @@
         tb[b] = acc
         pltpu.make_async_copy(tb.at[b], t_out.at[b], s_out.at[2, b]).start()
 
-    after = {
-        0: [lambda: yz_event(("L", 1, 0)), lambda: yz_event(("R", 1, 0))],
-        1: [lambda: x_event(("L", 1, 1)), lambda: x_event(("R", 1, 1)), lambda: x_relay(("R", 1, 1)), own_e2],
-        3: [lambda: yz_event(("L", 0, 1)), lambda: yz_event(("R", 0, 1))],
-        5: [wh_far],
-    }
-
-    def loop_a(b, _):
-        conv_step(b)
-        for k, todo in after.items():
-            @pl.when(b == k)
-            def _():
-                for f in todo:
-                    f()
-        return 0
-
-    lax.fori_loop(0, REQ, loop_a, 0)
-
-    loads[1].wait()
-    own_wh.wait()
+    loop(0, 5, conv_step, {
+        0: [("x", ("L", 0, 1)), ("x", ("R", 0, 1)), ("relay", ("R", 0, 1))],
+        1: [("yz", ("R", 1, 0))],
+        2: [("x", ("L", 1, 1)), ("x", ("R", 1, 1)), ("relay", ("R", 1, 1)), ("e2", own_e2)],
+        3: [("yz", ("L", 0, 1))],
+    })
+    wh_far()
+
+    loads[4].wait()
     for i in range(2, 4):
         arrived(hintb.at[:, 0], s_halo.at[i])
 
-    def h_step(b, _):
-        n = ids[b, 0]
+    def h_step(b):
+        n = ids[b]
         w = whs[n]
         v = jnp.dot(hintb[b].reshape(384, 192), w[0:192], preferred_element_type=F32)
         v = v + jnp.dot(lat48[b, :, 0:48], w[192:240], preferred_element_type=F32)
@@ -344,24 +380,26 @@
         hb[b] = v
         sums(sth.at[0], b, v)
         pltpu.make_async_copy(hb.at[b, pl.ds(64, 256)], h_out.at[b], s_out.at[1, b]).start()
-        return 0
-
-    lax.fori_loop(0, REQ, h_step, 0)
-
-    x_event(("LL", 0))
-    x_event(("RR", 0))
+
+    loop(0, REQ, h_step, {4: [("yz", ("R", 0, 1))]})
     stats_send(sth, 8, 0, "dz")
-    yz_event(("L", 1, 1))
-    yz_event(("R", 1, 1))
-    sth[4] = stats_sum(sth, 8, 0)
-    x_event(("LL", 1))
-    x_event(("RR", 1))
+    run([("x", ("LL", 0)), ("x", ("RR", 0))])
+
+    def stats_turn():
+        sth[4] = stats_sum(sth, 8, 0)
+
+    loop(5, REQ, conv_step, {
+        5: [("yz", ("L", 1, 1)), ("stats", stats_turn)],
+        6: [("x", ("LL", 1)), ("x", ("RR", 1))],
+        7: [("yz", ("R", 1, 1))],
+    })
     stats_send(sth, 8, 4, "dy")
     e2_event()
+    run([("yz", ("LL", 0))])
     stats_final(sth, 8)
 
-    def n_step(b, _):
-        n = ids[b, 0]
+    def n_step(b):
+        n = ids[b]
         gain = whs[n, 240:256, :][0:1].astype(F32)
         parts = [v.astype(BF16) for v in normed(hb[b], sth, b, gain)]
         for i, v in enumerate(parts):
@@ -369,16 +407,12 @@
         ntb[b] = jnp.concatenate([v[:, 256:320] for v in parts], axis=1)
         pltpu.make_async_copy(nmb.at[b], nm_out.at[b], s_out.at[3, b]).start()
         pltpu.make_async_copy(ntb.at[b], nt_out.at[b], s_out.at[4, b]).start()
-        @pl.when(b == 3)
-        def _():
-            yz_event(("LL", 0))
-            yz_event(("RR", 0))
-            e2_far()
-        return 0
-
-    lax.fori_loop(0, REQ, n_step, 0)
-    yz_event(("LL", 1))
-    yz_event(("RR", 1))
+
+    loop(0, REQ, n_step, {
+        2: [("yz", ("RR", 0))],
+        5: [("e2", e2_far), ("yz", ("LL", 1))],
+    })
+    run([("yz", ("RR", 1))])
 
     arrived(g.at[pl.ds(0, 4)], s_sib)
     arrived(g.at[pl.ds(0, 7)], s_send)
@@ -404,7 +438,7 @@
     lax.fori_loop(0, REQ, out_step, 0)
 
 
-def gather_call(ids, latf, hint, wh, wu, blob, ugain, uconv):
+def gather_call(*args):
     hbm = pl.BlockSpec(memory_space=pl.ANY)
     vm = pl.BlockSpec(memory_space=pltpu.VMEM)
     sm = pl.BlockSpec(memory_space=pltpu.SMEM)
@@ -419,13 +453,17 @@
             jax.ShapeDtypeStruct((REQ, 3, 384, 256), BF16),
             jax.ShapeDtypeStruct((REQ, 384, 192), BF16),
         ),
-        in_specs=[sm, vm, hbm, vm, vm, hbm, vm, hbm],
+        in_specs=[sm, vm, hbm, vm, hbm, vm, hbm, hbm, hbm, vm, vm, hbm],
         out_specs=(hbm,) * 6,
         scratch_shapes=[
             pltpu.VMEM((ROWS, 256), BF16),
             pltpu.VMEM((8, WHR, CH), BF16),
+            pltpu.VMEM((3, 3, CH, CH), BF16),
+            pltpu.VMEM((CH, CH), BF16),
+            pltpu.VMEM((CH, CH), BF16),
+            pltpu.VMEM((48, CH), BF16),
             pltpu.VMEM((REQ, 6, 64, 192), BF16),
-            pltpu.VMEM((4, 32, 256), F32),
+            pltpu.VMEM((2, REQ, 4, 256), BF16),
             pltpu.VMEM((REQ, 384, 128), BF16),
             pltpu.VMEM((REQ, 384, CH), BF16),
             pltpu.VMEM((REQ, 384, CH), BF16),
@@ -437,13 +475,13 @@
             pltpu.VMEM((9, 16, CH), F32),
             pltpu.VMEM((9, 16, CH), F32),
             dma((12,)), dma((48,)), dma((4,)), dma((4,)), dma, dma, dma, dma,
-            dma((4,)), dma((4,)), dma((16,)), dma((16,)), dma((5,)), dma((5, REQ)),
+            dma((4,)), dma((4,)), dma((16,)), dma((16,)), dma((7,)), dma((5, REQ)),
         ],
         compiler_params=pltpu.CompilerParams(
             collective_id=0, has_side_effects=True, vmem_limit_bytes=60 << 20
         ),
         name="gather",
-    )(ids, latf, hint, wh, wu, blob, ugain, uconv)
+    )(*args)
 
 
 def control_kernel(ids, scale, valid, wb, nm, nt, hb, ub, tb, o0, o1):
@@ -514,39 +552,17 @@
     )(ids, scale, valid, g, nm, nt, hb, ub, tb)
 
 
-def input_rows(w):
-    w = jnp.flip(w, axis=1).reshape(3, 12, CH)
-    return jnp.pad(w, ((0, 0), (0, 4), (0, 0))).reshape(48, CH)
-
-
-def pack(conv, z0, z1):
-    m, t = slice(0, 256), slice(256, CH)
-    wm = conv[:, :, m, m].reshape(2304, 256)
-    wk = conv[:, :, t, m].reshape(576, 256)
-    wn = conv[:, :, m, t].transpose(0, 2, 1, 3).reshape(3, 256, 192)
-    kt = conv[:, :, t, t].reshape(3, 192, 64)
-    zk = jnp.stack([z0[t, t], z1[t, t], jnp.zeros((64, 64), BF16)])
-    last = jnp.concatenate([kt, zk], axis=1)
-    wn = jnp.concatenate([wn, last], axis=2).reshape(768, 256)
-    zt = jnp.concatenate([z0[m, t], z1[m, t]], axis=1).reshape(2, 128, 128)
-    zt = jnp.concatenate([zt[0], zt[1]], axis=1)
-    return jnp.concatenate([wm, wk, wn, z1[:, m], z0[:, m], zt], axis=0)
-
-
 def shards(
     latent, hint, cond_ids, valid, cond_scale,
     ctl_in, ctl_hint, ctl_zero0, ctl_gain, ctl_conv, ctl_zero1,
     unet_in, unet_gain, unet_conv,
 ):
-    latf = latent.astype(F32).transpose(1, 0, 2).reshape(32, 256)
-    wh = jnp.concatenate(
-        [ctl_hint[0], input_rows(ctl_in[0]), ctl_gain, jnp.zeros((15, CH), BF16)], axis=0
+    ids = cond_ids[:, 0]
+    g, t, u, h, nm, nt = gather_call(
+        ids, latent, hint, ctl_in, ctl_hint, ctl_gain, ctl_conv, ctl_zero0, ctl_zero1,
+        unet_in, unet_gain, unet_conv,
     )
-    blob = pack(ctl_conv[0], ctl_zero0[0], ctl_zero1[0])
-    g, t, u, h, nm, nt = gather_call(
-        cond_ids, latf, hint, wh, input_rows(unet_in), blob, unet_gain[None], unet_conv
-    )
-    return control_call(cond_ids[:, 0], cond_scale, valid, g, nm, nt, h, u, t)
+    return control_call(ids, cond_scale, valid, g, nm, nt, h, u, t)
 
 
 def solution(mesh):

time: 107 us -> 83.9 us (0.78)
  local copies, waits for them, and re-layouts: 14.2 us -> 0 us
  Pallas kernels: 87.6 us -> 83 us
  other arithmetic: 3.6 us -> 0 us
    pallas_call x1, Pallas kernels: 71.3 us -> 66.5 us  [gather_call(): pl.pallas_call(gather_kernel, out_shape=(jax.ShapeDtypeStruct((8, ROWS, 2...]
    slice x5 -> x0, local copies, waits for them, and re-layouts: 4.39 us -> none  [the longest x1 1.69 us: pack(): wk = conv[:, :, t, m].reshape(576, 256)]
    unnamed x17 -> x0, local copies, waits for them, and re-layouts: 3.7 us -> none
    concatenate x4 -> x0, other arithmetic: 2.72 us -> none  [the longest x1 1.71 us: shards(): jnp.concatenate([ctl_hint[0], input_rows(ctl_in[0]), ctl_gain, jnp.zeros(...]
    rev x2 -> x0, local copies, waits for them, and re-layouts: 1.51 us -> none  [input_rows(): w = jnp.flip(w, axis=1).reshape(3, 12, CH)]
    broadcast_in_dim x2 -> x0, local copies, waits for them, and re-layouts: 1.4 us -> none  [the longest x1 1.4 us: shards(): unet_gain[None]]
where the time goes in v1:
time: 83.9 us; the launch traced here: 83.7 us
  Pallas kernels  83 us (99%)
    pallas_call x1, Pallas kernels, gather_call(): pl.pallas_call(gather_kernel, out_shape=(jax.ShapeDtypeStruct((8, ROWS, 2...  66.5 us
    pallas_call x1, Pallas kernels, control_call(): pl.pallas_call(control_kernel, out_shape=(out, out), grid_spec=pltpu.Pref...  16.5 us

profile of v1, /device:TPU:1, one launch (start us, length us, event | category | flops | bytes accessed | tf_op | source)
XLA Modules:
  0.0 83.7 jit_solution(3046449594455894778)
XLA Ops:
  0.6 66.5 %gather.1 = (bf16[8,4416,256]{2,1,0:T(8,128)(2,1)}, f32[8,256,320]{2,1,0:T(8,128)}, bf16[8,256,320]{2,1,0:T(8,128)(2,1)}, bf16[8,256,320]{2,1,0:T(8,128)(2,1)}, ...) custom-call(s32[8]{0:T(128)} %bitcast.1, bf16[8,4,256]{2,1,0:T(4,128)(2,1)} %lat.1, ...), custom_call_target="tpu_custom_call" | custom-call | tf_op jit(solution)/shard_map/gather/pallas_call | solution.py:446
  67.1 16.5 %control.1 = (bf16[8,4,64,320]{3,2,1,0:T(8,128)(2,1)}, bf16[8,4,64,320]{3,2,1,0:T(8,128)(2,1)}) custom-call(s32[8]{0:T(128)} %bitcast.2, f32[8]{0:T(128)} %scale.1, s32[8]{0:T(128)} %valid.1, bf16[8,4416,256]{2,1,0:T(8,128)(2,1)} %get-tuple-element.8.wb, bf16[8,3,384,256]{3,2,1,0:T(8,128)(2,1)} %get-tuple-element.9.nm, ...), custom_call_target="tpu_custom_call" | custom-call | tf_op jit(solution)/shard_map/control/pallas_call | solution.py:532

commit v2 on v1

--- a/solution.py
+++ b/solution.py
@@ -14,7 +14,7 @@
 REQ = 8
 EPS = 1e-5
 O_M, O_K, O_N, O_Z1, O_Z0, O_ZT, ROWS = 0, 2304, 2880, 3648, 3968, 4288, 4416
-CHUNK = 256
+CHUNK = 224
 E2 = 16 * CHUNK
 E2N = ROWS - E2
 E2H = E2N // 2
@@ -28,7 +28,7 @@
 def gather_kernel(
     ids, lat, hint, cin, chint, cgain, conv, z0, z1, uin, ugain, uconv,
     g, t_out, u_out, h_out, nm_out, nt_out,
-    blob, whs, cv, z0v, z1v, wu, hintb, latb, lat48, ub, hb, mb, tb, nmb, ntb, ucv, stu, sth,
+    blob, whs, cv, z0v, z1v, wu, hintb, latb, lat48, ub, hb, mb, tb, nmb, ntb, ucv, raw, st, fin,
     s_x, s_yz, s_e, s_wh, s_sib, s_whsib, s_send, s_whsend,
     s_halo, s_hsend, s_st, s_stsend, s_loc, s_out,
 ):
@@ -81,6 +81,123 @@
         whs[net, 192 + 16 * i : 208 + 16 * i, :] = input_rows(cin[0, i])
         wu[16 * i : 16 * i + 16, :] = input_rows(uin[i])
     whs[net, 240:256, :] = jnp.broadcast_to(cgain[...].astype(F32), (16, CH)).astype(BF16)
+
+    loads[3].wait()
+
+    pl.semaphore_wait(barrier, len(partners))
+
+    def send(src, dst, sem, where, ssem):
+        pltpu.make_async_remote_copy(
+            src_ref=src, dst_ref=dst, send_sem=ssem, recv_sem=sem,
+            device_id=where, device_id_type=MESH,
+        ).start()
+
+    def arrived(ref, sem):
+        pltpu.make_async_copy(ref, ref, sem).wait()
+
+    EV = {}
+    for q in range(2):
+        for h in range(2):
+            EV["L", q, h] = (3, q, h, q * 2 + h)
+            EV["R", q, h] = (1, q, h, 4 + q * 2 + h)
+        EV["LL", q] = (2, q, 0, 8 + q)
+        EV["RR", q] = (2, q, 1, 10 + q)
+
+    def rows_of(q, h, dy=0, dz=0):
+        start = pl.multiple_of((colour(q, dy, dz) * 2 + (q * 8 + h)) * CHUNK, CHUNK)
+        return pl.ds(start, CHUNK)
+
+    def own_chunk(q, h):
+        r = rows_of(q, h)
+        send(blob.at[r], g.at[net, r], s_x.at[EV["L", q, h][3]], dev(dx=1), s_send)
+        send(blob.at[r], g.at[net, r], s_x.at[EV["R", q, h][3]], dev(dx=3), s_send)
+
+    def x_relay(key):
+        dx, q, h, _ = EV[key]
+        ref = g.at[net_of(dx), rows_of(q, h)]
+        if key[0] == "L":
+            send(ref, ref, s_x.at[EV["LL", q][3]], dev(dx=1), s_send)
+        else:
+            send(ref, ref, s_x.at[EV["RR", q][3]], dev(dx=3), s_send)
+
+    def to_sib(ref):
+        send(ref, ref, s_sib, dev(dc=1), s_send)
+
+    def dirs(q, h):
+        main, other = ((0, 1), (2, 3)) if q == 0 else ((2, 3), (0, 1))
+        return main + (other[h],)
+
+    STEP = [dict(dy=1), dict(dy=3), dict(dz=1), dict(dz=3)]
+    BACK = [dict(dy=3), dict(dy=1), dict(dz=3), dict(dz=1)]
+
+    def x_event(key):
+        dx, q, h, sem = EV[key]
+        ref = g.at[net_of(dx), rows_of(q, h)]
+        arrived(ref, s_x.at[sem])
+        for d in dirs(q, h):
+            send(ref, ref, s_yz.at[d * 12 + sem], dev(**STEP[d]), s_send)
+        to_sib(ref)
+
+    def yz_event(key):
+        dx, q, h, sem = EV[key]
+        for d in dirs(q, h):
+            ref = g.at[net_of(dx), rows_of(q, h, **BACK[d])]
+            arrived(ref, s_yz.at[d * 12 + sem])
+            to_sib(ref)
+
+    e2r, e2h = pl.ds(E2, E2N), (pl.ds(E2, E2H), pl.ds(E2 + E2H, E2H))
+
+    def own_e2():
+        send(blob.at[e2r], g.at[net, e2r], s_e.at[0], dev(dx=1), s_send)
+        send(blob.at[e2r], g.at[net, e2r], s_e.at[1], dev(dx=3), s_send)
+
+    def e2_event():
+        for i, dx, to in ((0, 3, 1), (1, 1, 3)):
+            ref = g.at[net_of(dx), e2r]
+            arrived(ref, s_e.at[i])
+            half = g.at[net_of(dx), e2h[i]]
+            send(half, half, s_e.at[2 + i], dev(dx=to), s_send)
+            to_sib(ref)
+
+    def e2_far():
+        for i in range(2):
+            ref = g.at[net_of(2), e2h[i]]
+            arrived(ref, s_e.at[2 + i])
+            to_sib(ref)
+
+    whh = (pl.ds(0, WHR // 2), pl.ds(WHR // 2, WHR // 2))
+
+    def wh_sib(ref):
+        send(ref, ref, s_whsib, dev(dc=1), s_whsend)
+
+    def wh_event():
+        for i, dx, to in ((0, 3, 1), (1, 1, 3)):
+            ref = whs.at[net_of(dx)]
+            arrived(ref, s_wh.at[i])
+            half = whs.at[net_of(dx), whh[i]]
+            send(half, half, s_wh.at[2 + i], dev(dx=to), s_whsend)
+            wh_sib(ref)
+
+    def wh_far():
+        for i in range(2):
+            ref = whs.at[net_of(2), whh[i]]
+            arrived(ref, s_wh.at[2 + i])
+            wh_sib(ref)
+        arrived(whs.at[pl.ds(0, 4)], s_whsib)
+
+    halos = [
+        (lat, latb.at[0], rdev(1)), (lat, latb.at[1], rdev(15)),
+        (hint.at[:, 3], hintb.at[:, 0], rdev(1)), (hint.at[:, 0], hintb.at[:, 5], rdev(15)),
+    ]
+    for i, (src, dst, to) in enumerate(halos[:2]):
+        send(src, dst, s_halo.at[i], to, s_hsend.at[i])
+    mine = whs.at[net]
+    send(mine, mine, s_wh.at[0], dev(dx=1), s_whsend)
+    send(mine, mine, s_wh.at[1], dev(dx=3), s_whsend)
+    send(mine, mine, s_whsib, dev(dc=1), s_whsend)
+    for i, (src, dst, to) in enumerate(halos):
+        if i >= 2:
+            send(src, dst, s_halo.at[i], to, s_hsend.at[i])
 
     for cp in loads[:3]:
         cp.wait()
@@ -101,127 +218,32 @@
     blob[O_Z0 : O_Z0 + CH, :] = z0v[:, 0:256]
     zt = [zv[k : k + 128, 256:CH] for k in (0, 128) for zv in (z0v, z1v)]
     blob[O_ZT : O_ZT + 128, :] = jnp.concatenate(zt, axis=1)
-    loads[3].wait()
-
-    pl.semaphore_wait(barrier, len(partners))
-
-    def send(src, dst, sem, where, ssem):
-        pltpu.make_async_remote_copy(
-            src_ref=src, dst_ref=dst, send_sem=ssem, recv_sem=sem,
-            device_id=where, device_id_type=MESH,
-        ).start()
-
-    def arrived(ref, sem):
-        pltpu.make_async_copy(ref, ref, sem).wait()
-
-    EV = {}
-    for q in range(2):
-        for h in range(2):
-            EV["L", q, h] = (3, q, h, q * 2 + h)
-            EV["R", q, h] = (1, q, h, 4 + q * 2 + h)
-        EV["LL", q] = (2, q, 0, 8 + q)
-        EV["RR", q] = (2, q, 1, 10 + q)
-
-    def rows_of(q, h, dy=0, dz=0):
-        start = pl.multiple_of((colour(q, dy, dz) * 2 + (q * 8 + h)) * CHUNK, CHUNK)
-        return pl.ds(start, CHUNK)
-
-    def own_chunk(q, h):
-        r = rows_of(q, h)
-        send(blob.at[r], g.at[net, r], s_x.at[EV["L", q, h][3]], dev(dx=1), s_send)
-        send(blob.at[r], g.at[net, r], s_x.at[EV["R", q, h][3]], dev(dx=3), s_send)
-
-    def x_relay(key):
-        dx, q, h, _ = EV[key]
-        ref = g.at[net_of(dx), rows_of(q, h)]
-        if key[0] == "L":
-            send(ref, ref, s_x.at[EV["LL", q][3]], dev(dx=1), s_send)
-        else:
-            send(ref, ref, s_x.at[EV["RR", q][3]], dev(dx=3), s_send)
-
-    def to_sib(ref):
-        send(ref, ref, s_sib, dev(dc=1), s_send)
-
-    def dirs(q, h):
-        main, other = ((0, 1), (2, 3)) if q == 0 else ((2, 3), (0, 1))
-        return main + (other[h],)
-
-    STEP = [dict(dy=1), dict(dy=3), dict(dz=1), dict(dz=3)]
-    BACK = [dict(dy=3), dict(dy=1), dict(dz=3), dict(dz=1)]
-
-    def x_event(key):
-        dx, q, h, sem = EV[key]
-        ref = g.at[net_of(dx), rows_of(q, h)]
-        arrived(ref, s_x.at[sem])
-        for d in dirs(q, h):
-            send(ref, ref, s_yz.at[d * 12 + sem], dev(**STEP[d]), s_send)
-        to_sib(ref)
-
-    def yz_event(key):
-        dx, q, h, sem = EV[key]
-        for d in dirs(q, h):
-            ref = g.at[net_of(dx), rows_of(q, h, **BACK[d])]
-            arrived(ref, s_yz.at[d * 12 + sem])
-            to_sib(ref)
-
-    e2r, e2h = pl.ds(E2, E2N), (pl.ds(E2, E2H), pl.ds(E2 + E2H, E2H))
-
-    def own_e2():
-        send(blob.at[e2r], g.at[net, e2r], s_e.at[0], dev(dx=1), s_send)
-        send(blob.at[e2r], g.at[net, e2r], s_e.at[1], dev(dx=3), s_send)
-
-    def e2_event():
-        for i, dx, to in ((0, 3, 1), (1, 1, 3)):
-            ref = g.at[net_of(dx), e2r]
-            arrived(ref, s_e.at[i])
-            half = g.at[net_of(dx), e2h[i]]
-            send(half, half, s_e.at[2 + i], dev(dx=to), s_send)
-            to_sib(ref)
-
-    def e2_far():
-        for i in range(2):
-            ref = g.at[net_of(2), e2h[i]]
-            arrived(ref, s_e.at[2 + i])
-            to_sib(ref)
-
-    whh = (pl.ds(0, WHR // 2), pl.ds(WHR // 2, WHR // 2))
-
-    def wh_sib(ref):
-        send(ref, ref, s_whsib, dev(dc=1), s_whsend)
-
-    def wh_event():
-        for i, dx, to in ((0, 3, 1), (1, 1, 3)):
-            ref = whs.at[net_of(dx)]
-            arrived(ref, s_wh.at[i])
-            half = whs.at[net_of(dx), whh[i]]
-            send(half, half, s_wh.at[2 + i], dev(dx=to), s_whsend)
-            wh_sib(ref)
-
-    def wh_far():
-        for i in range(2):
-            ref = whs.at[net_of(2), whh[i]]
-            arrived(ref, s_wh.at[2 + i])
-            wh_sib(ref)
-        arrived(whs.at[pl.ds(0, 4)], s_whsib)
-
-    halos = [
-        (lat, latb.at[0], rdev(1)), (lat, latb.at[1], rdev(15)),
-        (hint.at[:, 3], hintb.at[:, 0], rdev(1)), (hint.at[:, 0], hintb.at[:, 5], rdev(15)),
-    ]
-    for i, (src, dst, to) in enumerate(halos[:2]):
-        send(src, dst, s_halo.at[i], to, s_hsend.at[i])
-    own_chunk(0, 0)
-    own_chunk(1, 0)
-    mine = whs.at[net]
-    send(mine, mine, s_wh.at[0], dev(dx=1), s_whsend)
-    send(mine, mine, s_wh.at[1], dev(dx=3), s_whsend)
-    send(mine, mine, s_whsib, dev(dc=1), s_whsend)
-    send(blob, g.at[net], s_sib, dev(dc=1), s_send)
-    for i, (src, dst, to) in enumerate(halos):
-        if i >= 2:
-            send(src, dst, s_halo.at[i], to, s_hsend.at[i])
     own_blob = pltpu.make_async_copy(blob, g.at[net], s_loc.at[6])
     own_blob.start()
+
+    def run(todo):
+        for name, key in todo:
+            if name == "x":
+                x_event(key)
+            elif name == "yz":
+                yz_event(key)
+            elif name == "relay":
+                x_relay(key)
+            elif name == "own":
+                own_chunk(*key)
+            else:
+                key()
+
+    def loop(first, last, piece, after):
+        def body(b, _):
+            piece(b)
+            for k, todo in after.items():
+                @pl.when(b == k)
+                def _():
+                    run(todo)
+            return 0
+
+        lax.fori_loop(first, last, body, 0)
 
     for i in range(2):
         arrived(latb.at[i], s_halo.at[i])
@@ -232,7 +254,7 @@
     ls = lax.broadcasted_iota(jnp.int32, (64, 128), 1)
     keep = (ls < 12) & ~((ls < 4) & (xs == 63)) & ~((ls >= 8) & (xs == 0))
 
-    def lat_step(b, _):
+    def lat_step(b):
         rolled = []
         above = jnp.where(rep > 0, latb[0, b].astype(F32)[2:4], 0.0)
         below = jnp.where(rep < 15, latb[1, b].astype(F32)[0:2], 0.0)
@@ -246,65 +268,81 @@
         for r in range(6):
             v = rolled[r] + pltpu.roll(rolled[r + 1], 16, 1) + pltpu.roll(rolled[r + 2], 32, 1)
             lat48[b, pl.ds(r * 64, 64), :] = v.astype(BF16)
-        return 0
-
-    lax.fori_loop(0, REQ, lat_step, 0)
-
-    def sums(st, b, v):
+
+    loop(0, REQ, lat_step, {
+        5: [("wh", wh_event)] + [("own", (q, h)) for h in range(2) for q in range(2)],
+    })
+
+    def sums(row, v):
         f = v[64:320].astype(F32)
-        st[pl.ds(b, 1), :] = jnp.sum(f, axis=0, keepdims=True)
-        st[pl.ds(8 + b, 1), :] = jnp.sum(f * f, axis=0, keepdims=True)
+        raw[pl.ds(row, 1), :] = jnp.sum(f, axis=0, keepdims=True)
+        raw[pl.ds(8 + row, 1), :] = jnp.sum(f * f, axis=0, keepdims=True)
 
     def u_step(b, _):
         v = jnp.dot(lat48[b, :, 0:48], wu[...], preferred_element_type=F32).astype(BF16)
         ub[b] = v
-        sums(stu.at[0], b, v)
+        sums(b, v)
         pltpu.make_async_copy(ub.at[b, pl.ds(64, 256)], u_out.at[b], s_out.at[0, b]).start()
         return 0
 
     lax.fori_loop(0, REQ, u_step, 0)
 
-    def stats_send(st, base, k, axis):
+    wh_far()
+    send(blob, g.at[net], s_sib, dev(dc=1), s_send)
+    loads[4].wait()
+    for i in range(2, 4):
+        arrived(hintb.at[:, 0], s_halo.at[i])
+
+    def h_step(b):
+        n = ids[b]
+        w = whs[n]
+        v = jnp.dot(hintb[b].reshape(384, 192), w[0:192], preferred_element_type=F32)
+        v = v + jnp.dot(lat48[b, :, 0:48], w[192:240], preferred_element_type=F32)
+        v = v.astype(BF16)
+        hb[b] = v
+        sums(16 + b, v)
+        pltpu.make_async_copy(hb.at[b, pl.ds(64, 256)], h_out.at[b], s_out.at[1, b]).start()
+
+    loop(0, REQ, h_step, {})
+
+    def stats_send(k, axis):
         for j in range(1, 4):
-            send(st.at[k], st.at[k + j], s_st.at[base + k + j], dev(**{axis: j}), s_stsend.at[base + k + j])
-
-    def stats_sum(st, base, k):
+            send(st.at[k], st.at[k + j], s_st.at[k + j], dev(**{axis: j}), s_stsend.at[k + j])
+
+    def stats_sum(k):
         total = st[k]
         for j in range(1, 4):
-            arrived(st.at[k + j], s_st.at[base + k + j])
+            arrived(st.at[k + j], s_st.at[k + j])
             total = total + st[k + j]
         return total
 
-    stats_send(stu, 0, 0, "dz")
-    x_event(("L", 0, 0))
-    x_event(("R", 0, 0))
-    own_chunk(0, 1)
-    stu[4] = stats_sum(stu, 0, 0)
-    x_event(("L", 1, 0))
-    stats_send(stu, 0, 4, "dy")
-    x_event(("R", 1, 0))
-    own_chunk(1, 1)
-
-    gi = lax.broadcasted_iota(jnp.int32, (CH, CH), 0)
-    gj = lax.broadcasted_iota(jnp.int32, (CH, CH), 1)
     gsz = CH // GROUPS
-    same = (lax.div(gi, gsz) == lax.div(gj, gsz)).astype(F32)
-
-    def stats_final(st, base):
-        total = stats_sum(st, base, 4)
-        per = jnp.dot(total, same, preferred_element_type=F32, precision=lax.Precision.HIGHEST)
-        per = per * (1.0 / (64 * 64 * gsz))
-        m, q = per[0:8], per[8:16]
-        st[8, 0:8, :] = m
-        st[8, 8:16, :] = lax.rsqrt(q - m * m + EPS)
+    gi = lax.broadcasted_iota(jnp.int32, (CH, 128), 0)
+    gj = lax.broadcasted_iota(jnp.int32, (CH, 128), 1)
+    member = (lax.div(gi, gsz) == gj).astype(F32)
+    st[0] = jnp.dot(raw[...], member, preferred_element_type=F32, precision=lax.Precision.HIGHEST)
+    stats_send(0, "dz")
+    st[4] = stats_sum(0)
+    stats_send(4, "dy")
+    run([("x", ("L", 0, 0)), ("x", ("R", 0, 0)), ("x", ("L", 1, 0)), ("x", ("R", 1, 0))])
+    run([("relay", ("L", 0, 0)), ("relay", ("L", 1, 0))])
+
+    per = stats_sum(4) * (1.0 / (64 * 64 * gsz))
+    for k in (0, 16):
+        m, q = per[k : k + 8], per[k + 8 : k + 16]
+        both = jnp.concatenate([m, lax.rsqrt(q - m * m + EPS)], axis=0)
+        fin[k : k + 16, :] = lax.dot_general(
+            both, member, (((1,), (1,)), ((), ())),
+            preferred_element_type=F32, precision=lax.Precision.HIGHEST,
+        )
 
     pos = lax.broadcasted_iota(jnp.int32, (384, CH), 0)
     col = lax.rem(pos, 64)
     inside = ((pos >= 64) | (rep > 0)) & ((pos < 320) | (rep < 15))
 
-    def normed(v, st, b, gain):
-        m = st[8, pl.ds(b, 1), :]
-        s = st[8, pl.ds(8 + b, 1), :] * gain
+    def normed(v, row, gain):
+        m = fin[pl.ds(row, 1), :]
+        s = fin[pl.ds(8 + row, 1), :] * gain
         n = (v.astype(F32) - m) * s
         n = n / (1.0 + jnp.exp(-n))
         n = jnp.where(inside, n, 0.0)
@@ -312,39 +350,15 @@
         right = jnp.where(col == 63, 0.0, pltpu.roll(n, 383, 0))
         return left, n, right
 
-    def run(todo):
-        for name, key in todo:
-            if name == "x":
-                x_event(key)
-            elif name == "yz":
-                yz_event(key)
-            elif name == "relay":
-                x_relay(key)
-            else:
-                key()
-
-    def loop(first, last, piece, after):
-        def body(b, _):
-            piece(b)
-            for k, todo in after.items():
-                @pl.when(b == k)
-                def _():
-                    run(todo)
-            return 0
-
-        lax.fori_loop(first, last, body, 0)
-
-    run([("yz", ("L", 0, 0))])
-    stats_final(stu, 0)
-
     def m_step(b):
-        for i, v in enumerate(normed(ub[b], stu, b, ugain[...].astype(F32).reshape(1, CH))):
+        for i, v in enumerate(normed(ub[b], b, ugain[...].astype(F32).reshape(1, CH))):
             mb[b, i] = v.astype(BF16)
 
     loop(0, REQ, m_step, {
-        2: [("yz", ("R", 0, 0))],
-        4: [("wh", wh_event), ("relay", ("L", 0, 0)), ("relay", ("L", 1, 0))],
-        7: [("yz", ("L", 1, 0))],
+        1: [("x", ("L", 0, 1)), ("x", ("R", 0, 1)), ("relay", ("R", 0, 1))],
+        3: [("yz", ("L", 0, 0))],
+        5: [("x", ("L", 1, 1)), ("x", ("R", 1, 1)), ("relay", ("R", 1, 1)), ("e2", own_e2)],
+        7: [("yz", ("R", 0, 0))],
     })
 
     loads[5].wait()
@@ -359,60 +373,29 @@
         tb[b] = acc
         pltpu.make_async_copy(tb.at[b], t_out.at[b], s_out.at[2, b]).start()
 
-    loop(0, 5, conv_step, {
-        0: [("x", ("L", 0, 1)), ("x", ("R", 0, 1)), ("relay", ("R", 0, 1))],
-        1: [("yz", ("R", 1, 0))],
-        2: [("x", ("L", 1, 1)), ("x", ("R", 1, 1)), ("relay", ("R", 1, 1)), ("e2", own_e2)],
-        3: [("yz", ("L", 0, 1))],
+    loop(0, REQ, conv_step, {
+        0: [("yz", ("L", 1, 0))],
+        1: [("x", ("LL", 0)), ("x", ("RR", 0))],
+        2: [("x", ("LL", 1)), ("x", ("RR", 1))],
+        3: [("yz", ("R", 1, 0))],
+        5: [("yz", ("L", 0, 1)), ("yz", ("L", 1, 1))],
+        7: [("yz", ("R", 0, 1)), ("yz", ("R", 1, 1))],
     })
-    wh_far()
-
-    loads[4].wait()
-    for i in range(2, 4):
-        arrived(hintb.at[:, 0], s_halo.at[i])
-
-    def h_step(b):
-        n = ids[b]
-        w = whs[n]
-        v = jnp.dot(hintb[b].reshape(384, 192), w[0:192], preferred_element_type=F32)
-        v = v + jnp.dot(lat48[b, :, 0:48], w[192:240], preferred_element_type=F32)
-        v = v.astype(BF16)
-        hb[b] = v
-        sums(sth.at[0], b, v)
-        pltpu.make_async_copy(hb.at[b, pl.ds(64, 256)], h_out.at[b], s_out.at[1, b]).start()
-
-    loop(0, REQ, h_step, {4: [("yz", ("R", 0, 1))]})
-    stats_send(sth, 8, 0, "dz")
-    run([("x", ("LL", 0)), ("x", ("RR", 0))])
-
-    def stats_turn():
-        sth[4] = stats_sum(sth, 8, 0)
-
-    loop(5, REQ, conv_step, {
-        5: [("yz", ("L", 1, 1)), ("stats", stats_turn)],
-        6: [("x", ("LL", 1)), ("x", ("RR", 1))],
-        7: [("yz", ("R", 1, 1))],
-    })
-    stats_send(sth, 8, 4, "dy")
-    e2_event()
-    run([("yz", ("LL", 0))])
-    stats_final(sth, 8)
 
     def n_step(b):
         n = ids[b]
         gain = whs[n, 240:256, :][0:1].astype(F32)
-        parts = [v.astype(BF16) for v in normed(hb[b], sth, b, gain)]
+        parts = [v.astype(BF16) for v in normed(hb[b], 16 + b, gain)]
         for i, v in enumerate(parts):
             nmb[b, i] = v[:, 0:256]
         ntb[b] = jnp.concatenate([v[:, 256:320] for v in parts], axis=1)
         pltpu.make_async_copy(nmb.at[b], nm_out.at[b], s_out.at[3, b]).start()
         pltpu.make_async_copy(ntb.at[b], nt_out.at[b], s_out.at[4, b]).start()
 
-    loop(0, REQ, n_step, {
-        2: [("yz", ("RR", 0))],
-        5: [("e2", e2_far), ("yz", ("LL", 1))],
-    })
-    run([("yz", ("RR", 1))])
+    loop(0, REQ, n_step, {7: [("yz", ("LL", 0))]})
+    e2_event()
+    run([("yz", ("RR", 0)), ("yz", ("LL", 1)), ("yz", ("RR", 1))])
+    e2_far()
 
     arrived(g.at[pl.ds(0, 4)], s_sib)
     arrived(g.at[pl.ds(0, 7)], s_send)
@@ -421,10 +404,9 @@
     for i in range(4):
         src = halos[i][0]
         pltpu.make_async_copy(src, src, s_hsend.at[i]).wait()
-    for base, st in ((0, stu), (8, sth)):
-        for k in (0, 4):
-            for j in range(1, 4):
-                arrived(st.at[k], s_stsend.at[base + k + j])
+    for k in (0, 4):
+        for j in range(1, 4):
+            arrived(st.at[k], s_stsend.at[k + j])
 
     def out_step(b, _):
         outs = (
@@ -472,10 +454,11 @@
             pltpu.VMEM((REQ, 3, 384, 256), BF16),
             pltpu.VMEM((REQ, 384, 192), BF16),
             pltpu.VMEM((3, 3, CH, CH), BF16),
-            pltpu.VMEM((9, 16, CH), F32),
-            pltpu.VMEM((9, 16, CH), F32),
+            pltpu.VMEM((32, CH), F32),
+            pltpu.VMEM((8, 32, 128), F32),
+            pltpu.VMEM((32, CH), F32),
             dma((12,)), dma((48,)), dma((4,)), dma((4,)), dma, dma, dma, dma,
-            dma((4,)), dma((4,)), dma((16,)), dma((16,)), dma((7,)), dma((5, REQ)),
+            dma((4,)), dma((4,)), dma((8,)), dma((8,)), dma((7,)), dma((5, REQ)),
         ],
         compiler_params=pltpu.CompilerParams(
             collective_id=0, has_side_effects=True, vmem_limit_bytes=60 << 20

time: 83.9 us -> 80.5 us (0.959)
  Pallas kernels: 83 us -> 79.6 us
    pallas_call x1, Pallas kernels: 66.5 us -> 63.1 us  [gather_call(): pl.pallas_call(gather_kernel, out_shape=(jax.ShapeDtypeStruct((8, ROWS, 2...]
where the time goes in v2:
time: 80.5 us; the launch traced here: 80.3 us
  Pallas kernels  79.6 us (99%)
    pallas_call x1, Pallas kernels, gather_call(): pl.pallas_call(gather_kernel, out_shape=(jax.ShapeDtypeStruct((8, ROWS, 2...  63.1 us
    pallas_call x1, Pallas kernels, control_call(): pl.pallas_call(control_kernel, out_shape=(out, out), grid_spec=pltpu.Pref...  16.5 us

profile of v2, /device:TPU:1, one launch (start us, length us, event | category | flops | bytes accessed | tf_op | source)
XLA Modules:
  0.0 80.3 jit_solution(15851754099124019354)
XLA Ops:
  0.6 63.1 %gather.1 = (bf16[8,4416,256]{2,1,0:T(8,128)(2,1)}, f32[8,256,320]{2,1,0:T(8,128)}, bf16[8,256,320]{2,1,0:T(8,128)(2,1)}, bf16[8,256,320]{2,1,0:T(8,128)(2,1)}, ...) custom-call(s32[8]{0:T(128)} %bitcast.1, bf16[8,4,256]{2,1,0:T(4,128)(2,1)} %lat.1, ...), custom_call_target="tpu_custom_call" | custom-call | tf_op jit(solution)/shard_map/gather/pallas_call | solution.py:428
  63.8 16.5 %control.1 = (bf16[8,4,64,320]{3,2,1,0:T(8,128)(2,1)}, bf16[8,4,64,320]{3,2,1,0:T(8,128)(2,1)}) custom-call(s32[8]{0:T(128)} %bitcast.2, f32[8]{0:T(128)} %scale.1, s32[8]{0:T(128)} %valid.1, bf16[8,4416,256]{2,1,0:T(8,128)(2,1)} %get-tuple-element.8.wb, bf16[8,3,384,256]{3,2,1,0:T(8,128)(2,1)} %get-tuple-element.9.nm, ...), custom_call_target="tpu_custom_call" | custom-call | tf_op jit(solution)/shard_map/control/pallas_call | solution.py:515

commit v3 on v2

--- a/solution.py
+++ b/solution.py
@@ -14,7 +14,7 @@
 REQ = 8
 EPS = 1e-5
 O_M, O_K, O_N, O_Z1, O_Z0, O_ZT, ROWS = 0, 2304, 2880, 3648, 3968, 4288, 4416
-CHUNK = 224
+CHUNK = 256
 E2 = 16 * CHUNK
 E2N = ROWS - E2
 E2H = E2N // 2
@@ -485,18 +485,17 @@
     r0 = proj(h0, O_Z0, 0, wb[0, O_N + 192 : O_N + 256, 192:256])
     o0[0] = (ub[0].astype(F32) + w * r0).astype(BF16).reshape(4, 64, CH)
 
-    main = jnp.zeros((256, 256), F32)
-    side = jnp.zeros((256, 192), F32)
+    rows = [slice(i * 64, i * 64 + 256) for i in range(3)]
+    lhs = jnp.concatenate([nm[0, j, r, :] for r in rows for j in range(3)], axis=1)
+    main = dot(lhs, wb[0, O_M:O_K, :])
+    lhs = jnp.concatenate([nm[0, 1, r, :] for r in rows], axis=1)
+    side = dot(lhs, wb[0, O_N:O_Z1, 0:192])
     tail = jnp.zeros((256, 64), F32)
     for i in range(3):
-        rows = slice(i * 64, i * 64 + 256)
-        for j in range(3):
-            k = O_M + (i * 3 + j) * 256
-            main = main + dot(nm[0, j, rows, :], wb[0, k : k + 256, :])
         k, n = O_K + i * 192, O_N + i * 256
-        main = main + dot(nt[0, rows, :], wb[0, k : k + 192, :])
-        side = side + dot(nm[0, 1, rows, :], wb[0, n : n + 256, 0:192])
-        tail = tail + dot(nt[0, rows, :], wb[0, n : n + 192, 192:256])
+        part = nt[0, rows[i], :]
+        main = main + dot(part, wb[0, k : k + 192, :])
+        tail = tail + dot(part, wb[0, n : n + 192, 192:256])
     col = lax.rem(lax.broadcasted_iota(jnp.int32, (256, 64), 0), 64)
     left = jnp.where(col == 0, 0.0, pltpu.roll(side[:, 0:64], 1, 0))
     right = jnp.where(col == 63, 0.0, pltpu.roll(side[:, 128:192], 255, 0))

time: 80.5 us -> 78.6 us (0.976)
  Pallas kernels: 79.6 us -> 77.7 us
    pallas_call x1, Pallas kernels: 63.1 us -> 61.2 us  [gather_call(): pl.pallas_call(gather_kernel, out_shape=(jax.ShapeDtypeStruct((8, ROWS, 2...]
where the time goes in v3:
time: 78.6 us; the launch traced here: 78.4 us
  Pallas kernels  77.7 us (99%)
    pallas_call x1, Pallas kernels, gather_call(): pl.pallas_call(gather_kernel, out_shape=(jax.ShapeDtypeStruct((8, ROWS, 2...  61.2 us
    pallas_call x1, Pallas kernels, control_call(): pl.pallas_call(control_kernel, out_shape=(out, out), grid_spec=pltpu.Pref...  16.5 us

profile of v3, /device:TPU:1, one launch (start us, length us, event | category | flops | bytes accessed | tf_op | source)
XLA Modules:
  0.0 78.4 jit_solution(13812779666153790377)
XLA Ops:
  0.6 61.2 %gather.1 = (bf16[8,4416,256]{2,1,0:T(8,128)(2,1)}, f32[8,256,320]{2,1,0:T(8,128)}, bf16[8,256,320]{2,1,0:T(8,128)(2,1)}, bf16[8,256,320]{2,1,0:T(8,128)(2,1)}, ...) custom-call(s32[8]{0:T(128)} %bitcast.1, bf16[8,4,256]{2,1,0:T(4,128)(2,1)} %lat.1, ...), custom_call_target="tpu_custom_call" | custom-call | tf_op jit(solution)/shard_map/gather/pallas_call | solution.py:428
  61.9 16.5 %control.1 = (bf16[8,4,64,320]{3,2,1,0:T(8,128)(2,1)}, bf16[8,4,64,320]{3,2,1,0:T(8,128)(2,1)}) custom-call(s32[8]{0:T(128)} %bitcast.2, f32[8]{0:T(128)} %scale.1, s32[8]{0:T(128)} %valid.1, bf16[8,4416,256]{2,1,0:T(8,128)(2,1)} %get-tuple-element.8.wb, bf16[8,3,384,256]{3,2,1,0:T(8,128)(2,1)} %get-tuple-element.9.nm, ...), custom_call_target="tpu_custom_call" | custom-call | tf_op jit(solution)/shard_map/control/pallas_call | solution.py:514
